TPU v7x, 512 devices: a whole 4x8x8 slice. The times are simulated.
512 devices in a mesh: orb: 32 (over y_hi, x, core), grp: 16 (over y_lo, z).
Axes of the slice: x: 4, y: 8 (y_hi: 4, y_lo: 2; y = y_hi * 2 + y_lo), z: 8, core: 2. Of those that a mesh axis runs over, the one named last changes fastest.
Arguments:
- orbitals: bfloat16 [512, 64000], P(('orb', 'grp')), may hold values from -8 to 8
Outputs:
- projector: bfloat16 [512, 64000], P(('orb', 'grp'))
All inputs are finite; a program needn't handle non-finite values.
Results may differ from a plain program's by a relative error of at most 0.0012.
The roundings to bfloat16 on the way count: a program that leaves them out, or rounds other values in their place, can miss the bound.
Values may be sent and summed in bfloat16 or wider, within the bound.
No kernel may reach another device: no remote copies, remote signals or barrier semaphores. Data moves between devices by JAX's collectives and lax.ppermute only.
A program may use at most 64 MiB of HBM per device.

v0:
```python
import math
import numpy as np
import jax
import jax.numpy as jnp
from jax import lax
from jax.experimental import pallas as pl
from jax.experimental.pallas import tpu as pltpu
from jax.sharding import Mesh
from jax.sharding import PartitionSpec as P


GRID = 40
CELLS = GRID**3
F32 = jnp.float32
BF16 = jnp.bfloat16


def cosine_sums(values, size):
    half = size // 2
    out = [None] * (half + 1)
    if size % 4 == 0:
        mid = half // 2
        folded = [values[x] + values[half - x] for x in range(mid)] + [values[mid]]
        for b, term in enumerate(cosine_sums(folded, half)):
            out[2 * b] = term
        rest = [values[x] - values[half - x] for x in range(mid)]
        for a in range(1, half + 1, 2):
            out[a] = weighted(rest, [math.cos(2 * math.pi * (a * x % size) / size) for x in range(mid)])
    else:
        for a in range(half + 1):
            out[a] = weighted(values, [math.cos(2 * math.pi * (a * x % size) / size) for x in range(half + 1)])
    return out


def sine_sums(values, size):
    half = size // 2
    out = [None] * (half + 1)
    if size % 4 == 0:
        mid = half // 2
        folded = [None] + [values[x] - values[half - x] for x in range(1, mid)]
        for b, term in enumerate(sine_sums(folded, half)):
            if term is not None:
                out[2 * b] = term
        rest = [values[x] + values[half - x] for x in range(1, mid)] + [values[mid]]
        for a in range(1, half, 2):
            out[a] = weighted(rest, [math.sin(2 * math.pi * (a * x % size) / size) for x in range(1, mid + 1)])
    else:
        for a in range(1, half):
            out[a] = weighted(values[1:half], [math.sin(2 * math.pi * (a * x % size) / size) for x in range(1, half)])
    return out


def weighted(values, weights):
    groups = {}
    for value, weight in zip(values, weights, strict=True):
        size = round(abs(weight), 12)
        if size == 0.0:
            continue
        groups.setdefault(size, []).append(value if weight > 0 else (value,))
    total = None
    for size, members in groups.items():
        part = None
        for m in members:
            if isinstance(m, tuple):
                part = -m[0] if part is None else part - m[0]
            else:
                part = m if part is None else part + m
        part = part if size == 1.0 else part * size
        total = part if total is None else total + part
    return total


def hartley(values):
    size = len(values)
    half = size // 2
    even = [values[0]] + [values[x] + values[size - x] for x in range(1, half)] + [values[half]]
    odd = [None] + [values[x] - values[size - x] for x in range(1, half)]
    cosines, sines = cosine_sums(even, size), sine_sums(odd, size)
    out = [None] * size
    out[0], out[half] = cosines[0], cosines[half]
    for a in range(1, half):
        out[a] = cosines[a] + sines[a]
        out[size - a] = cosines[a] - sines[a]
    return out


def split(x):
    high = x.astype(BF16)
    return high, (x - high.astype(F32)).astype(BF16)


def along_lanes(x, table_high, table_low):
    high, low = split(x)
    out = jnp.dot(high, table_high, preferred_element_type=F32)
    out += jnp.dot(low, table_high, preferred_element_type=F32)
    return out + jnp.dot(high, table_low, preferred_element_type=F32)


ROWS = 200


def exchange_kernel(o_ref, a_ref, b_ref, table_ref, kernel_ref, out_ref, field, sources):
    high, low = table_ref[0], table_ref[1]

    @pl.loop(0, GRID * GRID // ROWS)
    def _(step):
        rows = pl.ds(pl.multiple_of(step * ROWS, 8), ROWS)
        o = o_ref[rows, :].astype(F32)
        three = jnp.concatenate(
            [o, a_ref[rows, :].astype(F32), b_ref[rows, :].astype(F32), jnp.zeros((ROWS, 8), F32)], axis=1
        )
        target = jnp.concatenate([o, o, o, jnp.zeros((ROWS, 8), F32)], axis=1)
        sources[rows, :] = three
        field[rows, :] = along_lanes(target * three, high, low)

    @pl.loop(0, GRID // 8)
    def _(chunk):
        rows = [pl.ds(pl.multiple_of(GRID * x + 8 * chunk, 8), 8) for x in range(GRID)]
        for x, value in enumerate(hartley([field[r, :] for r in rows])):
            field[rows[x], :] = value

    @pl.loop(0, GRID // 8)
    def _(chunk):
        rows = [pl.ds(y + GRID * 8 * chunk, 8, stride=GRID) for y in range(GRID)]
        spectrum = hartley([field[r, :] for r in rows])
        around = pl.ds(pl.multiple_of(8 * chunk, 8), 8)
        spectrum = [v * kernel_ref[min(b, GRID - b), around, :] for b, v in enumerate(spectrum)]
        for y, value in enumerate(hartley(spectrum)):
            field[rows[y], :] = value

    @pl.loop(0, GRID // 8)
    def _(chunk):
        rows = [pl.ds(pl.multiple_of(GRID * x + 8 * chunk, 8), 8) for x in range(GRID)]
        for x, value in enumerate(hartley([field[r, :] for r in rows])):
            field[rows[x], :] = value

    @pl.loop(0, GRID * GRID // ROWS)
    def _(step):
        rows = pl.ds(pl.multiple_of(step * ROWS, 8), ROWS)
        terms = sources[rows, :] * along_lanes(field[rows, :], high, low)
        total = terms + pltpu.roll(terms, 128 - GRID, axis=1) + pltpu.roll(terms, 128 - 2 * GRID, axis=1)
        out_ref[rows, :] = (-total[:, :GRID]).astype(BF16)


def hartley_tables():
    index = np.arange(GRID)
    angle = 2 * np.pi / GRID * (index[:, None] * index[None, :] % GRID)
    cas = (np.cos(angle) + np.sin(angle)).astype(np.float32)
    table = np.zeros((128, 128), np.float32)
    for s in range(3):
        table[GRID * s : GRID * (s + 1), GRID * s : GRID * (s + 1)] = cas
    high = jnp.asarray(table).astype(BF16)
    low = (jnp.asarray(table) - high.astype(F32)).astype(BF16)
    return jnp.stack([high, low])


def kernel_table():
    freq = np.arange(GRID)
    wave = 2 * np.pi / GRID * np.where(freq <= GRID // 2, freq, freq - GRID)
    square = wave * wave
    total = square[: GRID // 2 + 1, None, None] + square[None, :, None] + square[None, None, :]
    safe = np.where(total > 0, total, 1.0)
    table = np.where(total > 0, 4 * (1 - np.exp(-0.25 * total)) / safe, 1.0) / CELLS
    out = np.zeros((GRID // 2 + 1, GRID, 128), np.float32)
    for s in range(3):
        out[:, :, GRID * s : GRID * (s + 1)] = table
    return jnp.asarray(out)


def exchange_of(o, a, b):
    square = GRID * GRID
    return pl.pallas_call(
        exchange_kernel,
        out_shape=jax.ShapeDtypeStruct((square, GRID), BF16),
        in_specs=[pl.BlockSpec(memory_space=pltpu.VMEM)] * 5,
        out_specs=pl.BlockSpec(memory_space=pltpu.VMEM),
        scratch_shapes=[pltpu.VMEM((square, 128), F32), pltpu.VMEM((square, 128), F32)],
        compiler_params=pltpu.CompilerParams(vmem_limit_bytes=32 << 20),
        cost_estimate=pl.CostEstimate(flops=10_000_000, bytes_accessed=4_000_000, transcendentals=0),
        name="exchange",
    )(o.reshape(square, GRID), a.reshape(square, GRID), b.reshape(square, GRID), hartley_tables(), kernel_table())


N = 512
BLOCK = 128


def thirds(x):
    high = x.astype(BF16)
    rest = x - high.astype(F32)
    middle = rest.astype(BF16)
    return high, middle, (rest - middle.astype(F32)).astype(BF16)


def exact_dot(a, b):
    (a0, a1, a2), (b0, b1, b2) = thirds(a), thirds(b)
    d = lambda p, q: jnp.dot(p, q, preferred_element_type=F32)
    return d(a0, b0) + (d(a0, b1) + d(a1, b0)) + (d(a1, b1) + d(a0, b2) + d(a2, b0))


def invert_block(groups):
    sub = lax.broadcasted_iota(jnp.int32, (8, BLOCK), 0)
    lane = lax.broadcasted_iota(jnp.int32, (8, BLOCK), 1)
    wide = lambda x, j: jnp.broadcast_to(x[j : j + 1, :], (8, BLOCK))
    for p in range(BLOCK // 8):
        here = (lane >= 8 * p) & (lane < 8 * p + 8)
        column = lambda v, k: jnp.broadcast_to(groups[v][:, 8 * p + k : 8 * p + k + 1], (8, BLOCK))
        pivots = [column(p, k) for k in range(8)]
        below = {v: [column(v, k) for k in range(8)] for v in range(p + 1, BLOCK // 8)}
        panel = jnp.where(here, jnp.where(lane - 8 * p == sub, 1.0, 0.0), groups[p])
        lower = jnp.zeros((8, BLOCK), F32)
        scale = jnp.zeros((8, BLOCK), F32)
        for j in range(8):
            r = 1.0 / wide(pivots[j], j)
            factor = jnp.where(sub == j, 0.0, pivots[j])
            row = wide(panel, j)
            lower = jnp.where(sub == j, row, lower)
            scale = jnp.where(sub == j, r, scale)
            for k in range(j + 1, 8):
                pivots[k] = pivots[k] - (factor * wide(pivots[k], j)) * r
            panel = panel - (factor * row) * r
        panel = panel * scale
        groups[p] = lower * jnp.sqrt(scale)
        spread = [wide(panel, k) for k in range(8)]
        for v in range(p + 1, BLOCK // 8):
            value = jnp.where(here, 0.0, groups[v])
            for k in range(8):
                value = value - below[v][k] * spread[k]
            groups[v] = value
    return groups


def factor_kernel(place_ref, parts_ref, out_ref, m, w):
    core, column, block = place_ref[0], place_ref[1], place_ref[2]
    for r in range(4):
        for q in range(4):
            for p in range(4):
                top = BLOCK * p + 32 * q
                part = parts_ref[(p // 2) ^ core, 4 * r + q, 32 * (p % 2) : 32 * (p % 2) + 32, :]
                m[top : top + 32, BLOCK * r : BLOCK * (r + 1)] = part
    rows = lambda i: slice(BLOCK * i, BLOCK * (i + 1))
    eye = lax.broadcasted_iota(jnp.int32, (BLOCK, BLOCK), 0) == lax.broadcasted_iota(jnp.int32, (BLOCK, BLOCK), 1)
    sums = [jnp.zeros((1, BLOCK), F32) for _ in range(4)]
    trace = jnp.zeros((1, BLOCK), F32)
    for i in range(4):
        for j in range(i + 1):
            s = (m[rows(i), rows(j)] + m[rows(j), rows(i)].T) * (-0.5 / CELLS)
            flipped = s.T
            m[rows(i), rows(j)] = s
            sums[j] = sums[j] + jnp.sum(jnp.abs(s), axis=0, keepdims=True)
            if i != j:
                m[rows(j), rows(i)] = flipped
                sums[i] = sums[i] + jnp.sum(jnp.abs(flipped), axis=0, keepdims=True)
            else:
                trace = trace + jnp.sum(jnp.where(eye, jnp.abs(s), 0.0), axis=0, keepdims=True)
    gamma = jnp.sum(trace, axis=1, keepdims=True) / N + 1e-6
    for i in range(4):
        m[rows(i), rows(i)] = m[rows(i), rows(i)] + jnp.where(eye, sums[i] + gamma, 0.0)

    @pl.loop(0, 4)
    def _(s):
        here = pl.ds(pl.multiple_of(s * BLOCK, BLOCK), BLOCK)
        groups = [m[pl.ds(pl.multiple_of(s * BLOCK + 8 * v, 8), 8), here] for v in range(BLOCK // 8)]
        for v, value in enumerate(invert_block(groups)):
            w[8 * v : 8 * v + 8, :] = value
        lower = lax.broadcasted_iota(jnp.int32, (BLOCK, BLOCK), 0) >= lax.broadcasted_iota(jnp.int32, (BLOCK, BLOCK), 1)
        inverse = jnp.where(lower, w[...], 0.0)
        m[here, :] = exact_dot(inverse, m[here, :])
        m[here, here] = inverse
        for i in range(1, 4):

            @pl.when(i > s)
            def _():
                left = m[here, rows(i)].T
                m[rows(i), here] = jnp.zeros((BLOCK, BLOCK), F32)
                m[rows(i), :] = m[rows(i), :] - exact_dot(left, m[here, :])

    mine = pl.ds(pl.multiple_of(32 * block, 32), 32)
    row = lax.broadcasted_iota(jnp.int32, (32, BLOCK), 0) + 32 * block
    lane = lax.broadcasted_iota(jnp.int32, (32, BLOCK), 1)
    values = [jnp.where(lane + BLOCK * p <= row, m[mine, BLOCK * p : BLOCK * (p + 1)], 0.0) for p in range(4)]
    for k in range(4):
        s = lax.rem(column + 4 - k, 4)
        total = jnp.zeros((32, BLOCK), F32)
        for p, value in enumerate(values):
            turned = pltpu.roll(value, lax.rem(p + 4 - s, 4) * 32, axis=1)
            total = jnp.where(lane // 32 == p, turned, total)
        out_ref[k] = total.astype(BF16)


def inverse_rows(place, parts):
    return pl.pallas_call(
        factor_kernel,
        out_shape=jax.ShapeDtypeStruct((4, 32, BLOCK), BF16),
        in_specs=[pl.BlockSpec(memory_space=pltpu.SMEM), pl.BlockSpec(memory_space=pltpu.VMEM)],
        out_specs=pl.BlockSpec(memory_space=pltpu.VMEM),
        scratch_shapes=[pltpu.VMEM((N, N), F32), pltpu.VMEM((BLOCK, BLOCK), F32)],
        compiler_params=pltpu.CompilerParams(vmem_limit_bytes=32 << 20),
        cost_estimate=pl.CostEstimate(flops=400_000_000, bytes_accessed=4_000_000, transcendentals=0),
        name="factor",
    )(place, parts)


AXES = ("yh", "x", "c", "yl", "z")
BLOCKS = ("yh", "x", "c")
SLABS = ("c", "yl", "z")
SHELF = ("yl", "z")
PLANE = ("yh", "x")


def shifted(value, axes, steps):
    count = lax.axis_size(axes)
    return lax.ppermute(value, axes, [(i, (i + steps) % count) for i in range(count)])


def swapped(tiles, axes):
    return lax.all_to_all(tiles, axes, split_axis=0, concat_axis=0, tiled=True)


def shown_to(value, axes):
    return swapped(jnp.broadcast_to(value, (lax.axis_size(axes), *value.shape)), axes)


def gathered_slab(row, axis):
    slabs, copies = lax.axis_size(SLABS), lax.axis_size(axis)
    tiles = jnp.broadcast_to(row.reshape(1, slabs, 2, -1), (copies, slabs, 2, CELLS // slabs // 2))
    return swapped(tiles.reshape(copies * slabs, 2, -1), (axis, *SLABS)).reshape(copies * slabs, -1)


def around(value, axes, way):
    pieces = [value]
    for k in range(1, lax.axis_size(axes)):
        pieces.append(shifted(value, axes, way * k))
    return pieces


def steps(orbitals):
    slabs = lax.axis_size(SLABS)
    width = CELLS // slabs
    first, second = shifted(orbitals, BLOCKS, 1), shifted(orbitals, BLOCKS, 2)
    orbital_rows = gathered_slab(orbitals, "x")
    exchange = exchange_of(orbitals, first, second)
    exchange_rows = gathered_slab(exchange, "yh")
    margin = lax.dot_general(
        exchange_rows, orbital_rows, (((1,), (1,)), ((), ())), preferred_element_type=F32
    )
    summed = jnp.sum(swapped(margin.reshape(slabs, BLOCK // slabs, BLOCK), SLABS), axis=0)
    half = shown_to(summed, SHELF).reshape(BLOCK // 2, BLOCK)
    mine = shown_to(half, PLANE)
    other = shifted(mine, ("c",), 1)
    place = jnp.stack([lax.axis_index("c"), lax.axis_index("x"), lax.axis_index(PLANE)]).astype(jnp.int32)
    rows = inverse_rows(place, jnp.stack([mine, other]))
    projected = jnp.zeros((slabs, width), F32)
    for k, piece in enumerate(around(exchange_rows, ("x",), 1)):
        projected += jnp.dot(rows[k], piece, preferred_element_type=F32)
    return swapped(projected.astype(BF16).reshape(slabs, 2, -1), SLABS).reshape(1, CELLS)


def solution(mesh):
    split_mesh = Mesh(mesh.devices.reshape(4, 4, 2, 2, 8), AXES)
    placed = P(AXES, None)
    return jax.shard_map(steps, mesh=split_mesh, in_specs=placed, out_specs=placed, check_vma=False)
```

profile of v0, /device:TPU:1, one launch (start us, length us, event | category | flops | bytes accessed | tf_op | source)
XLA Modules:
  0.0 184.0 jit_solution(11999471781371905125)
XLA Ops:
  0.0 1.7 reduce
  1.7 0.2 broadcast_in_dim.22
  1.9 0.1 broadcast_in_dim.23
  1.9 1.3 copy.19
  3.3 16.8 %all-to-all-start.1 = ((bf16[128,2,1000]{2,1,0:T(2,128)(2,1)}), bf16[128,2,1000]{2,1,0:T(2,128)(2,1)S(1)}, u32[]{:S(2)}, u32[]{:S(2)}) async-start(bf16[128,2,1000]{2,1,0:T(2,128)(2,1)} %copy.19), calls=%async_computation.1 | async-start | bytes 1048576 | tf_op jit(solution)/shard_map/all_to_all | solution.py:317
  20.1 3.6 %collective-permute-start = (bf16[1,64000]{1,0:T(2,128)(2,1)S(1)}, bf16[1,64000]{1,0:T(2,128)(2,1)S(1)}, u32[]{:S(2)}, u32[]{:S(2)}) collective-permute-start(bf16[1,64000]{1,0:T(2,128)(2,1)S(1)} %copy-done.2), channel_id=1, source_target_pairs={{0,16},{16,32},{32,48},{48,64},{64,80},{80,96},{96,112},{112,128},... | collective-permute-start | bytes 384008 | tf_op jit(solution)/shard_map/ppermute | solution.py:313
  23.7 3.3 %collective-permute-start.1 = (bf16[1,64000]{1,0:T(2,128)(2,1)S(1)}, bf16[1,64000]{1,0:T(2,128)(2,1)S(1)}, u32[]{:S(2)}, u32[]{:S(2)}) collective-permute-start(bf16[1,64000]{1,0:T(2,128)(2,1)S(1)} %copy-done.2), channel_id=1, source_target_pairs={{0,32},{16,48},{32,64},{48,80},{64,96},{80,112},{96,128},{112,144}... | collective-permute-start | bytes 384008 | tf_op jit(solution)/shard_map/ppermute | solution.py:313
  27.0 0.6 reshape.37.o_ref
  27.6 3.7 %collective-permute-done = bf16[1,64000]{1,0:T(2,128)(2,1)S(1)} collective-permute-done((bf16[1,64000]{1,0:T(2,128)(2,1)S(1)}, bf16[1,64000]{1,0:T(2,128)(2,1)S(1)}, u32[]{:S(2)}, u32[]{:S(2)}) %collective-permute-start) | collective-permute-done | bytes 128032 | tf_op jit(solution)/shard_map/ppermute | solution.py:313
  31.4 0.7 reduce.1
  32.1 0.6 reshape.38.a_ref
  32.7 0.0 copy-start
  32.7 18.5 %collective-permute-done.1 = bf16[1,64000]{1,0:T(2,128)(2,1)S(1)} collective-permute-done((bf16[1,64000]{1,0:T(2,128)(2,1)S(1)}, bf16[1,64000]{1,0:T(2,128)(2,1)S(1)}, u32[]{:S(2)}, u32[]{:S(2)}) %collective-permute-start.1) | collective-permute-done | bytes 128032 | tf_op jit(solution)/shard_map/ppermute | solution.py:313
  51.2 0.8 reduce.2
  52.0 0.0 copy-start.1
  52.0 0.6 reshape.39.b_ref
  52.7 0.2 copy-done.1
  52.9 6.7 %exchange.1 = bf16[1600,40]{1,0:T(8,128)(2,1)S(1)} custom-call(bf16[1600,40]{1,0:T(8,128)(2,1)S(1)} %reshape.37.o_ref, bf16[1600,40]{1,0:T(8,128)(2,1)S(1)} %reshape.38.a_ref, bf16[1600,40]{1,0:T(8,128)(2,1)S(1)} %reshape.39.b_ref, bf16[2,128,128]{2,1,0:T(8,128)(2,1)S(1)} %copy-done.1, f32[21,40,128]{2,1,0:T(8,128)S(1)} %copy-done), custom_call_target="tpu_custom_call" | custom-call | flops 10000000 | bytes 4000000 | tf_op jit(solution)/shard_map/exchange/pallas_call | solution.py:172
  59.5 0.4 broadcast_in_dim.20
  60.0 0.1 broadcast_in_dim.21
  60.1 1.3 copy.17
  61.4 0.0 all-to-all-done.1
  61.4 9.5 %all-to-all-start = ((bf16[128,2,1000]{2,1,0:T(2,128)(2,1)}), bf16[128,2,1000]{2,1,0:T(2,128)(2,1)S(1)}, u32[]{:S(2)}, u32[]{:S(2)}) async-start(bf16[128,2,1000]{2,1,0:T(2,128)(2,1)} %copy.17), calls=%async_computation | async-start | bytes 1048576 | tf_op jit(solution)/shard_map/all_to_all | solution.py:317
  70.9 0.7 copy.20
  71.7 18.6 %all-to-all-done = bf16[128,2,1000]{2,1,0:T(2,128)(2,1)S(1)} async-done(((bf16[128,2,1000]{2,1,0:T(2,128)(2,1)}), bf16[128,2,1000]{2,1,0:T(2,128)(2,1)S(1)}, u32[]{:S(2)}, u32[]{:S(2)}) %all-to-all-start) | async-done | bytes 512032 | tf_op jit(solution)/shard_map/all_to_all | solution.py:317
  90.3 0.6 dot_general.17
  90.9 0.4 fusion.2
  91.4 13.1 %all_to_all.30 = f32[32,4,128]{2,1,0:T(4,128)S(1)} all-to-all(f32[32,4,128]{2,1,0:T(4,128)S(1)} %copy.22), channel_id=1, replica_groups=mesh['yh'=4,'x'=4,'c'=2,'yl'=2,'z'=8] {'c','yl','z'}, dimensions={0} | all-to-all | bytes 131072 | tf_op jit(solution)/shard_map/all_to_all | solution.py:317
  104.6 9.9 %all_to_all.31 = f32[16,4,128]{2,1,0:T(4,128)S(1)} all-to-all(f32[16,4,128]{2,1,0:T(4,128)S(1)} %broadcast_in_dim.24), channel_id=1, replica_groups=mesh['yh'=4,'x'=4,'c'=2,'yl'=2,'z'=8] {'yl','z'}, dimensions={0} | all-to-all | bytes 65536 | tf_op jit(solution)/shard_map/all_to_all | solution.py:317
  114.5 18.9 %all_to_all.32 = f32[16,64,128]{2,1,0:T(8,128)S(1)} all-to-all(f32[16,64,128]{2,1,0:T(8,128)S(1)} %broadcast_in_dim.25), channel_id=1, replica_groups=mesh['yh'=4,'x'=4,'c'=2,'yl'=2,'z'=8] {'yh','x'}, dimensions={0} | all-to-all | bytes 1048576 | tf_op jit(solution)/shard_map/all_to_all | solution.py:317
  133.5 4.2 %collective-permute-start.2 = (f32[16,64,128]{2,1,0:T(8,128)S(1)}, f32[16,64,128]{2,1,0:T(8,128)S(1)}, u32[]{:S(2)}, u32[]{:S(2)}) collective-permute-start(f32[16,64,128]{2,1,0:T(8,128)S(1)} %all_to_all.32), channel_id=1, source_target_pairs={{0,16},{16,0},{1,17},{17,1},{2,18},{18,2},{3,19},{19,3},{4,20},{20... | collective-permute-start | bytes 1572872 | tf_op jit(solution)/shard_map/ppermute | solution.py:313
  137.7 0.7 copy.23
  138.5 3.1 %collective-permute-start.5 = (bf16[128,2000]{0,1:T(8,128)(2,1)S(1)}, bf16[128,2000]{0,1:T(8,128)(2,1)S(1)}, u32[]{:S(2)}, u32[]{:S(2)}) collective-permute-start(bf16[128,2000]{0,1:T(8,128)(2,1)S(1)} %bitcast.32), channel_id=1, source_target_pairs={{0,96},{32,0},{64,32},{96,64},{1,97},{33,1},{65,33},{97,65},{2,98}... | collective-permute-start | bytes 1536008 | tf_op jit(solution)/shard_map/ppermute | solution.py:313
  141.6 0.1 pad_add_fusion.place_ref
  141.7 2.2 %collective-permute-start.3 = (bf16[128,2000]{0,1:T(8,128)(2,1)S(1)}, bf16[128,2000]{0,1:T(8,128)(2,1)S(1)}, u32[]{:S(2)}, u32[]{:S(2)}) collective-permute-start(bf16[128,2000]{0,1:T(8,128)(2,1)S(1)} %bitcast.33), channel_id=1, source_target_pairs={{0,32},{32,64},{64,96},{96,0},{1,33},{33,65},{65,97},{97,1},{2,34}... | collective-permute-start | bytes 1536008 | tf_op jit(solution)/shard_map/ppermute | solution.py:313
  143.8 3.4 %collective-permute-start.4 = (bf16[128,2000]{0,1:T(8,128)(2,1)S(1)}, bf16[128,2000]{0,1:T(8,128)(2,1)S(1)}, u32[]{:S(2)}, u32[]{:S(2)}) collective-permute-start(bf16[128,2000]{0,1:T(8,128)(2,1)S(1)} %bitcast.34), channel_id=1, source_target_pairs={{0,64},{32,96},{64,0},{96,32},{1,65},{33,97},{65,1},{97,33},{2,66}... | collective-permute-start | bytes 1536008 | tf_op jit(solution)/shard_map/ppermute | solution.py:313
  147.3 0.1 pad_maximum_fusion.parts_ref
  147.4 22.3 %factor.1 = bf16[4,32,128]{2,1,0:T(8,128)(2,1)S(1)} custom-call(s32[3]{0:T(128)S(1)} %pad_add_fusion.place_ref, f32[2,16,64,128]{3,2,1,0:T(8,128)S(1)} %pad_maximum_fusion.parts_ref), custom_call_target="tpu_custom_call" | custom-call | flops 400000000 | bytes 4000000 | tf_op jit(solution)/shard_map/factor/pallas_call | solution.py:292
  169.7 0.3 fusion.5
  170.0 0.0 collective-permute-done.5
  170.0 0.3 fusion.4
  170.3 0.0 collective-permute-done.3
  170.3 0.3 convolution_add_fusion.1
  170.6 0.0 collective-permute-done.4
  170.6 0.3 fusion.1
  170.9 0.2 reshape.45
  171.1 11.9 %all_to_all.33 = bf16[32,2,1000]{2,1,0:T(2,128)(2,1)S(1)} all-to-all(bf16[32,2,1000]{2,1,0:T(2,128)(2,1)S(1)} %reshape.45), channel_id=1, replica_groups=mesh['yh'=4,'x'=4,'c'=2,'yl'=2,'z'=8] {'c','yl','z'}, dimensions={0} | all-to-all | bytes 256000 | tf_op jit(solution)/shard_map/all_to_all | solution.py:317
  183.0 1.0 reshape.46
  (10 shorter events, 0.2 us)
Async XLA Ops:
  3.3 16.8 %copy-start.2 = (bf16[1,64000]{1,0:T(2,128)(2,1)S(1)}, bf16[1,64000]{1,0:T(2,128)(2,1)}, u32[]{:S(2)}) copy-start(bf16[1,64000]{1,0:T(2,128)(2,1)} %param.3) | copy-start | bytes 384004
  3.3 58.1 %all-to-all-start.1 = ((bf16[128,2,1000]{2,1,0:T(2,128)(2,1)}), bf16[128,2,1000]{2,1,0:T(2,128)(2,1)S(1)}, u32[]{:S(2)}, u32[]{:S(2)}) async-start(bf16[128,2,1000]{2,1,0:T(2,128)(2,1)} %copy.19), calls=%async_computation.1 | async-start | bytes 1048576 | tf_op jit(solution)/shard_map/all_to_all | solution.py:317
  20.1 11.3 %collective-permute-start = (bf16[1,64000]{1,0:T(2,128)(2,1)S(1)}, bf16[1,64000]{1,0:T(2,128)(2,1)S(1)}, u32[]{:S(2)}, u32[]{:S(2)}) collective-permute-start(bf16[1,64000]{1,0:T(2,128)(2,1)S(1)} %copy-done.2), channel_id=1, source_target_pairs={{0,16},{16,32},{32,48},{48,64},{64,80},{80,96},{96,112},{112,128},... | collective-permute-start | bytes 384008 | tf_op jit(solution)/shard_map/ppermute | solution.py:313
  23.7 27.5 %collective-permute-start.1 = (bf16[1,64000]{1,0:T(2,128)(2,1)S(1)}, bf16[1,64000]{1,0:T(2,128)(2,1)S(1)}, u32[]{:S(2)}, u32[]{:S(2)}) collective-permute-start(bf16[1,64000]{1,0:T(2,128)(2,1)S(1)} %copy-done.2), channel_id=1, source_target_pairs={{0,32},{16,48},{32,64},{48,80},{64,96},{80,112},{96,128},{112,144}... | collective-permute-start | bytes 384008 | tf_op jit(solution)/shard_map/ppermute | solution.py:313
  32.7 19.9 %copy-start = (f32[21,40,128]{2,1,0:T(8,128)S(1)}, f32[21,40,128]{2,1,0:T(8,128)}, u32[]{:S(2)}) copy-start(f32[21,40,128]{2,1,0:T(8,128)} %constant.25.clone.kernel_ref) | copy-start | bytes 1290244
  52.0 0.8 copy-start.1
  61.4 28.9 %all-to-all-start = ((bf16[128,2,1000]{2,1,0:T(2,128)(2,1)}), bf16[128,2,1000]{2,1,0:T(2,128)(2,1)S(1)}, u32[]{:S(2)}, u32[]{:S(2)}) async-start(bf16[128,2,1000]{2,1,0:T(2,128)(2,1)} %copy.17), calls=%async_computation | async-start | bytes 1048576 | tf_op jit(solution)/shard_map/all_to_all | solution.py:317
  133.5 13.8 %collective-permute-start.2 = (f32[16,64,128]{2,1,0:T(8,128)S(1)}, f32[16,64,128]{2,1,0:T(8,128)S(1)}, u32[]{:S(2)}, u32[]{:S(2)}) collective-permute-start(f32[16,64,128]{2,1,0:T(8,128)S(1)} %all_to_all.32), channel_id=1, source_target_pairs={{0,16},{16,0},{1,17},{17,1},{2,18},{18,2},{3,19},{19,3},{4,20},{20... | collective-permute-start | bytes 1572872 | tf_op jit(solution)/shard_map/ppermute | solution.py:313
  138.5 31.5 %collective-permute-start.5 = (bf16[128,2000]{0,1:T(8,128)(2,1)S(1)}, bf16[128,2000]{0,1:T(8,128)(2,1)S(1)}, u32[]{:S(2)}, u32[]{:S(2)}) collective-permute-start(bf16[128,2000]{0,1:T(8,128)(2,1)S(1)} %bitcast.32), channel_id=1, source_target_pairs={{0,96},{32,0},{64,32},{96,64},{1,97},{33,1},{65,33},{97,65},{2,98}... | collective-permute-start | bytes 1536008 | tf_op jit(solution)/shard_map/ppermute | solution.py:313
  141.7 28.6 %collective-permute-start.3 = (bf16[128,2000]{0,1:T(8,128)(2,1)S(1)}, bf16[128,2000]{0,1:T(8,128)(2,1)S(1)}, u32[]{:S(2)}, u32[]{:S(2)}) collective-permute-start(bf16[128,2000]{0,1:T(8,128)(2,1)S(1)} %bitcast.33), channel_id=1, source_target_pairs={{0,32},{32,64},{64,96},{96,0},{1,33},{33,65},{65,97},{97,1},{2,34}... | collective-permute-start | bytes 1536008 | tf_op jit(solution)/shard_map/ppermute | solution.py:313
  143.8 26.8 %collective-permute-start.4 = (bf16[128,2000]{0,1:T(8,128)(2,1)S(1)}, bf16[128,2000]{0,1:T(8,128)(2,1)S(1)}, u32[]{:S(2)}, u32[]{:S(2)}) collective-permute-start(bf16[128,2000]{0,1:T(8,128)(2,1)S(1)} %bitcast.34), channel_id=1, source_target_pairs={{0,64},{32,96},{64,0},{96,32},{1,65},{33,97},{65,1},{97,33},{2,66}... | collective-permute-start | bytes 1536008 | tf_op jit(solution)/shard_map/ppermute | solution.py:313
where the time goes:
time: 185 us; the launch traced here: 184 us
  blocking collectives  53.9 us (29%)
  starting transfers between devices  46.2 us (25%)
  waiting for transfers between devices  40.9 us (22%)
  Pallas kernels  29 us (16%)
  local copies, waits for them, and re-layouts  8.84 us (5%)
  other arithmetic  3.37 us (2%)
    all_to_all x4, blocking collectives, swapped(): return lax.all_to_all(tiles, axes, split_axis=0, concat_axis=0, tiled=True)  53.9 us
    all_to_all x2, starting transfers between devices, swapped(): return lax.all_to_all(tiles, axes, split_axis=0, concat_axis=0, tiled=True)  26.3 us
    pallas_call x1, Pallas kernels, inverse_rows(): pl.pallas_call(factor_kernel, out_shape=jax.ShapeDtypeStruct((4, 32, BLOC...  22.3 us
    ppermute x6, waiting for transfers between devices, shifted(): lax.ppermute(value, axes, [(i, (i + steps) % count) for i in range(count)])  22.2 us
    ppermute x6, starting transfers between devices, shifted(): lax.ppermute(value, axes, [(i, (i + steps) % count) for i in range(count)])  19.9 us
    all_to_all x2, waiting for transfers between devices, swapped(): return lax.all_to_all(tiles, axes, split_axis=0, concat_axis=0, tiled=True)  18.7 us
    pallas_call x1, Pallas kernels, exchange_of(): pl.pallas_call(exchange_kernel, out_shape=jax.ShapeDtypeStruct((square, G...  6.66 us
  transfers between devices with their start and end apart: 8, of which 3 were waited for; matrix products, arithmetic and copies ran while one was open for 4% of the time, Pallas kernels for 16%

commit v1 on v0

--- a/solution.py
+++ b/solution.py
@@ -193,8 +193,15 @@
 
 
 def exact_dot(a, b):
+    (a0, a1, a2), (b0, b1, b2) = a, b
+    top = jnp.concatenate([b0, b1], axis=0)
+    d = lambda p, q, r: jnp.dot(jnp.concatenate([p, q], axis=1), r, preferred_element_type=F32)
+    return d(a0, a0, top) + (d(a1, a1, top) + d(a0, a2, jnp.concatenate([b2, b0], axis=0)))
+
+
+def exact_dot_t(a, b):
     (a0, a1, a2), (b0, b1, b2) = thirds(a), thirds(b)
-    d = lambda p, q: jnp.dot(p, q, preferred_element_type=F32)
+    d = lambda p, q: lax.dot_general(p, q, (((1,), (1,)), ((), ())), preferred_element_type=F32)
     return d(a0, b0) + (d(a0, b1) + d(a1, b0)) + (d(a1, b1) + d(a0, b2) + d(a2, b0))
 
 
@@ -202,42 +209,52 @@
     sub = lax.broadcasted_iota(jnp.int32, (8, BLOCK), 0)
     lane = lax.broadcasted_iota(jnp.int32, (8, BLOCK), 1)
     wide = lambda x, j: jnp.broadcast_to(x[j : j + 1, :], (8, BLOCK))
-    for p in range(BLOCK // 8):
-        here = (lane >= 8 * p) & (lane < 8 * p + 8)
-        column = lambda v, k: jnp.broadcast_to(groups[v][:, 8 * p + k : 8 * p + k + 1], (8, BLOCK))
-        pivots = [column(p, k) for k in range(8)]
-        below = {v: [column(v, k) for k in range(8)] for v in range(p + 1, BLOCK // 8)}
-        panel = jnp.where(here, jnp.where(lane - 8 * p == sub, 1.0, 0.0), groups[p])
-        lower = jnp.zeros((8, BLOCK), F32)
-        scale = jnp.zeros((8, BLOCK), F32)
-        for j in range(8):
-            r = 1.0 / wide(pivots[j], j)
-            factor = jnp.where(sub == j, 0.0, pivots[j])
-            row = wide(panel, j)
-            lower = jnp.where(sub == j, row, lower)
-            scale = jnp.where(sub == j, r, scale)
-            for k in range(j + 1, 8):
-                pivots[k] = pivots[k] - (factor * wide(pivots[k], j)) * r
-            panel = panel - (factor * row) * r
-        panel = panel * scale
-        groups[p] = lower * jnp.sqrt(scale)
-        spread = [wide(panel, k) for k in range(8)]
-        for v in range(p + 1, BLOCK // 8):
-            value = jnp.where(here, 0.0, groups[v])
-            for k in range(8):
-                value = value - below[v][k] * spread[k]
+    size = 16
+    count = size // 8
+    pair = range(count)
+    for p in range(BLOCK // size):
+        first = size * p
+        here = (lane >= first) & (lane < first + size)
+        column = lambda v, k: jnp.broadcast_to(groups[v][:, first + k : first + k + 1], (8, BLOCK))
+        pivots = [[column(count * p + g, k) for g in pair] for k in range(size)]
+        panel = [
+            jnp.where(here, jnp.where(lane - first - 8 * g == sub, 1.0, 0.0), groups[count * p + g]) for g in pair
+        ]
+        lower = [jnp.zeros((8, BLOCK), F32) for _ in pair]
+        scale = [jnp.zeros((8, BLOCK), F32) for _ in pair]
+        for j in range(size):
+            gj, sj = j // 8, j % 8
+            r = 1.0 / wide(pivots[j][gj], sj)
+            factor = [(jnp.where(sub == sj, 0.0, pivots[j][g]) if g == gj else pivots[j][g]) * r for g in pair]
+            row = wide(panel[gj], sj)
+            lower[gj] = jnp.where(sub == sj, row, lower[gj])
+            scale[gj] = jnp.where(sub == sj, r, scale[gj])
+            for k in range(j + 1, size):
+                across = wide(pivots[k][gj], sj)
+                pivots[k] = [pivots[k][g] - factor[g] * across for g in pair]
+            panel = [panel[g] - factor[g] * row for g in pair]
+        panel = [panel[g] * scale[g] for g in pair]
+        for g in pair:
+            groups[count * p + g] = lower[g] * jnp.sqrt(scale[g])
+        spread = [wide(panel[k // 8], k % 8) for k in range(size)]
+        for v in range(count * (p + 1), BLOCK // 8):
+            parts = [column(v, k) * spread[k] for k in range(size)]
+            while len(parts) > 1:
+                parts = [a + b for a, b in zip(parts[::2], parts[1::2])]
+            value = jnp.where(here, 0.0, groups[v]) - parts[0]
             groups[v] = value
     return groups
 
 
-def factor_kernel(place_ref, parts_ref, out_ref, m, w):
-    core, column, block = place_ref[0], place_ref[1], place_ref[2]
+def factor_kernel(place_ref, parts_ref, out_ref, m, w, x):
+    core, shelf, column, block = place_ref[0], place_ref[1], place_ref[2], place_ref[3]
     for r in range(4):
         for q in range(4):
             for p in range(4):
                 top = BLOCK * p + 32 * q
-                part = parts_ref[(p // 2) ^ core, 4 * r + q, 32 * (p % 2) : 32 * (p % 2) + 32, :]
-                m[top : top + 32, BLOCK * r : BLOCK * (r + 1)] = part
+                m[top : top + 32, BLOCK * r : BLOCK * (r + 1)] = parts_ref[
+                    (p // 2) ^ core, 4 * r + q, 32 * (p % 2) : 32 * (p % 2) + 32, :
+                ]
     rows = lambda i: slice(BLOCK * i, BLOCK * (i + 1))
     eye = lax.broadcasted_iota(jnp.int32, (BLOCK, BLOCK), 0) == lax.broadcasted_iota(jnp.int32, (BLOCK, BLOCK), 1)
     sums = [jnp.zeros((1, BLOCK), F32) for _ in range(4)]
@@ -245,45 +262,57 @@
     for i in range(4):
         for j in range(i + 1):
             s = (m[rows(i), rows(j)] + m[rows(j), rows(i)].T) * (-0.5 / CELLS)
-            flipped = s.T
-            m[rows(i), rows(j)] = s
             sums[j] = sums[j] + jnp.sum(jnp.abs(s), axis=0, keepdims=True)
             if i != j:
+                flipped = s.T
                 m[rows(j), rows(i)] = flipped
                 sums[i] = sums[i] + jnp.sum(jnp.abs(flipped), axis=0, keepdims=True)
             else:
+                m[rows(i), rows(i)] = s
                 trace = trace + jnp.sum(jnp.where(eye, jnp.abs(s), 0.0), axis=0, keepdims=True)
     gamma = jnp.sum(trace, axis=1, keepdims=True) / N + 1e-6
     for i in range(4):
         m[rows(i), rows(i)] = m[rows(i), rows(i)] + jnp.where(eye, sums[i] + gamma, 0.0)
+    keep = lax.broadcasted_iota(jnp.int32, (BLOCK, BLOCK), 0) >= lax.broadcasted_iota(jnp.int32, (BLOCK, BLOCK), 1)
 
     @pl.loop(0, 4)
-    def _(s):
-        here = pl.ds(pl.multiple_of(s * BLOCK, BLOCK), BLOCK)
-        groups = [m[pl.ds(pl.multiple_of(s * BLOCK + 8 * v, 8), 8), here] for v in range(BLOCK // 8)]
+    def _(step):
+        here = pl.ds(pl.multiple_of(step * BLOCK, BLOCK), BLOCK)
+        groups = [m[pl.ds(pl.multiple_of(step * BLOCK + 8 * v, 8), 8), here] for v in range(BLOCK // 8)]
         for v, value in enumerate(invert_block(groups)):
             w[8 * v : 8 * v + 8, :] = value
-        lower = lax.broadcasted_iota(jnp.int32, (BLOCK, BLOCK), 0) >= lax.broadcasted_iota(jnp.int32, (BLOCK, BLOCK), 1)
-        inverse = jnp.where(lower, w[...], 0.0)
-        m[here, :] = exact_dot(inverse, m[here, :])
-        m[here, here] = inverse
-        for i in range(1, 4):
-
-            @pl.when(i > s)
+        m[here, here] = jnp.where(keep, w[...], 0.0)
+        for s in range(3):
+
+            @pl.when(step == s)
             def _():
-                left = m[here, rows(i)].T
-                m[rows(i), here] = jnp.zeros((BLOCK, BLOCK), F32)
-                m[rows(i), :] = m[rows(i), :] - exact_dot(left, m[here, :])
-
+                start = BLOCK * (s + 1)
+                right = exact_dot(thirds(m[rows(s), rows(s)]), thirds(m[rows(s), start:]))
+                m[rows(s), start:] = right
+                pieces = thirds(right)
+                for i in range(s + 1, 4):
+                    begin = BLOCK * (i - s - 1)
+                    left = thirds(right[:, begin : begin + BLOCK].T)
+                    m[rows(i), BLOCK * i :] = m[rows(i), BLOCK * i :] - exact_dot(left, [t[:, begin:] for t in pieces])
+
+    x[...] = jnp.zeros_like(x)
     mine = pl.ds(pl.multiple_of(32 * block, 32), 32)
-    row = lax.broadcasted_iota(jnp.int32, (32, BLOCK), 0) + 32 * block
+    own = pl.ds(pl.multiple_of(BLOCK * shelf, BLOCK), BLOCK)
+    x[:, own] = m[mine, own]
+    for j in (2, 1, 0):
+
+        @pl.when(j < shelf)
+        def _():
+            start = BLOCK * (j + 1)
+            total = exact_dot_t(x[:, start:], m[rows(j), start:])
+            x[:, rows(j)] = -exact_dot(thirds(total), thirds(m[rows(j), rows(j)]))
+
     lane = lax.broadcasted_iota(jnp.int32, (32, BLOCK), 1)
-    values = [jnp.where(lane + BLOCK * p <= row, m[mine, BLOCK * p : BLOCK * (p + 1)], 0.0) for p in range(4)]
     for k in range(4):
         s = lax.rem(column + 4 - k, 4)
         total = jnp.zeros((32, BLOCK), F32)
-        for p, value in enumerate(values):
-            turned = pltpu.roll(value, lax.rem(p + 4 - s, 4) * 32, axis=1)
+        for p in range(4):
+            turned = pltpu.roll(x[:, rows(p)], lax.rem(p + 4 - s, 4) * 32, axis=1)
             total = jnp.where(lane // 32 == p, turned, total)
         out_ref[k] = total.astype(BF16)
 
@@ -294,7 +323,7 @@
         out_shape=jax.ShapeDtypeStruct((4, 32, BLOCK), BF16),
         in_specs=[pl.BlockSpec(memory_space=pltpu.SMEM), pl.BlockSpec(memory_space=pltpu.VMEM)],
         out_specs=pl.BlockSpec(memory_space=pltpu.VMEM),
-        scratch_shapes=[pltpu.VMEM((N, N), F32), pltpu.VMEM((BLOCK, BLOCK), F32)],
+        scratch_shapes=[pltpu.VMEM((N, N), F32), pltpu.VMEM((BLOCK, BLOCK), F32), pltpu.VMEM((32, N), F32)],
         compiler_params=pltpu.CompilerParams(vmem_limit_bytes=32 << 20),
         cost_estimate=pl.CostEstimate(flops=400_000_000, bytes_accessed=4_000_000, transcendentals=0),
         name="factor",
@@ -304,8 +333,8 @@
 AXES = ("yh", "x", "c", "yl", "z")
 BLOCKS = ("yh", "x", "c")
 SLABS = ("c", "yl", "z")
-SHELF = ("yl", "z")
-PLANE = ("yh", "x")
+QUARTER = ("c", "yl")
+PLANE = ("yh", "x", "yl")
 
 
 def shifted(value, axes, steps):
@@ -321,10 +350,17 @@
     return swapped(jnp.broadcast_to(value, (lax.axis_size(axes), *value.shape)), axes)
 
 
-def gathered_slab(row, axis):
+def gathered_slab(row, axis, last):
     slabs, copies = lax.axis_size(SLABS), lax.axis_size(axis)
-    tiles = jnp.broadcast_to(row.reshape(1, slabs, 2, -1), (copies, slabs, 2, CELLS // slabs // 2))
-    return swapped(tiles.reshape(copies * slabs, 2, -1), (axis, *SLABS)).reshape(copies * slabs, -1)
+    tiles = row.reshape(slabs, 2, -1)
+    if last:
+        tiles = jnp.broadcast_to(tiles[:, None], (slabs, copies, *tiles.shape[1:]))
+        tiles = swapped(tiles.reshape(slabs * copies, *tiles.shape[2:]), (*SLABS, axis))
+        tiles = jnp.swapaxes(tiles.reshape(slabs, copies, *tiles.shape[1:]), 0, 1)
+    else:
+        tiles = jnp.broadcast_to(tiles[None], (copies, *tiles.shape))
+        tiles = swapped(tiles.reshape(copies * slabs, *tiles.shape[2:]), (axis, *SLABS))
+    return tiles.reshape(copies * slabs, -1)
 
 
 def around(value, axes, way):
@@ -338,17 +374,17 @@
     slabs = lax.axis_size(SLABS)
     width = CELLS // slabs
     first, second = shifted(orbitals, BLOCKS, 1), shifted(orbitals, BLOCKS, 2)
-    orbital_rows = gathered_slab(orbitals, "x")
+    orbital_rows = gathered_slab(orbitals, "x", True)
     exchange = exchange_of(orbitals, first, second)
-    exchange_rows = gathered_slab(exchange, "yh")
+    exchange_rows = gathered_slab(exchange, "yh", False)
     margin = lax.dot_general(
         exchange_rows, orbital_rows, (((1,), (1,)), ((), ())), preferred_element_type=F32
     )
-    summed = jnp.sum(swapped(margin.reshape(slabs, BLOCK // slabs, BLOCK), SLABS), axis=0)
-    half = shown_to(summed, SHELF).reshape(BLOCK // 2, BLOCK)
-    mine = shown_to(half, PLANE)
+    summed = jnp.sum(swapped(margin.reshape(4, BLOCK // 4, BLOCK), QUARTER), axis=0)
+    summed = jnp.sum(shown_to(summed, ("z",)), axis=0)
+    mine = shown_to(summed, PLANE).reshape(16, BLOCK // 2, BLOCK)
     other = shifted(mine, ("c",), 1)
-    place = jnp.stack([lax.axis_index("c"), lax.axis_index("x"), lax.axis_index(PLANE)]).astype(jnp.int32)
+    place = jnp.stack([lax.axis_index(a) for a in ("c", "yh", "x", ("yh", "x"))]).astype(jnp.int32)
     rows = inverse_rows(place, jnp.stack([mine, other]))
     projected = jnp.zeros((slabs, width), F32)
     for k, piece in enumerate(around(exchange_rows, ("x",), 1)):

time: 185 us -> 179 us (0.968)
  Pallas kernels: 29 us -> 22.2 us
  blocking collectives: 53.9 us -> 47.1 us
  waiting for transfers between devices: 40.9 us -> 46.1 us
  starting transfers between devices: 46.2 us -> 49.1 us
    pallas_call x1, Pallas kernels: 22.3 us -> 15.5 us  [inverse_rows(): pl.pallas_call(factor_kernel, out_shape=jax.ShapeDtypeStruct((4, 32, BLOC...]
    all_to_all x4, blocking collectives: 53.9 us -> 47.1 us  [swapped(): return lax.all_to_all(tiles, axes, split_axis=0, concat_axis=0, tiled=True)]
    ppermute x6, waiting for transfers between devices: 22.2 us -> 27.6 us  [shifted(): lax.ppermute(value, axes, [(i, (i + steps) % count) for i in range(count)])]
    ppermute x6, starting transfers between devices: 19.9 us -> 22.6 us  [shifted(): lax.ppermute(value, axes, [(i, (i + steps) % count) for i in range(count)])]
  transfers between devices with their start and end apart: 8 -> 8, of which waited for: 3 -> 5; matrix products, arithmetic and copies ran while one was open for 4% -> 4% of each run, Pallas kernels for 16% -> 12%
where the time goes in v1:
time: 179 us; the launch traced here: 178 us
  starting transfers between devices  49.1 us (27%)
  blocking collectives  47.1 us (26%)
  waiting for transfers between devices  46.1 us (26%)
  Pallas kernels  22.2 us (12%)
  local copies, waits for them, and re-layouts  8.68 us (5%)
  other arithmetic  3.35 us (2%)
    all_to_all x4, blocking collectives, swapped(): return lax.all_to_all(tiles, axes, split_axis=0, concat_axis=0, tiled=True)  47.1 us
    ppermute x6, waiting for transfers between devices, shifted(): lax.ppermute(value, axes, [(i, (i + steps) % count) for i in range(count)])  27.6 us
    all_to_all x2, starting transfers between devices, swapped(): return lax.all_to_all(tiles, axes, split_axis=0, concat_axis=0, tiled=True)  26.4 us
    ppermute x6, starting transfers between devices, shifted(): lax.ppermute(value, axes, [(i, (i + steps) % count) for i in range(count)])  22.6 us
    all_to_all x2, waiting for transfers between devices, swapped(): return lax.all_to_all(tiles, axes, split_axis=0, concat_axis=0, tiled=True)  18.4 us
    pallas_call x1, Pallas kernels, inverse_rows(): pl.pallas_call(factor_kernel, out_shape=jax.ShapeDtypeStruct((4, 32, BLOC...  15.5 us
    pallas_call x1, Pallas kernels, exchange_of(): pl.pallas_call(exchange_kernel, out_shape=jax.ShapeDtypeStruct((square, G...  6.66 us
  transfers between devices with their start and end apart: 8, of which 5 were waited for; matrix products, arithmetic and copies ran while one was open for 4% of the time, Pallas kernels for 12%

profile of v1, /device:TPU:1, one launch (start us, length us, event | category | flops | bytes accessed | tf_op | source)
XLA Modules:
  0.0 178.3 jit_solution(15999406981984647565)
XLA Ops:
  0.0 1.7 reduce
  1.7 0.2 broadcast_in_dim.22
  1.9 1.1 broadcast_in_dim.23
  2.9 17.1 %all-to-all-start.1 = ((bf16[128,2,1000]{2,1,0:T(2,128)(2,1)}), bf16[128,2,1000]{2,1,0:T(2,128)(2,1)S(1)}, u32[]{:S(2)}, u32[]{:S(2)}) async-start(bf16[128,2,1000]{2,1,0:T(2,128)(2,1)} %bitcast.5), calls=%async_computation.1 | async-start | bytes 1048576 | tf_op jit(solution)/shard_map/all_to_all | solution.py:346
  20.0 3.2 %collective-permute-start = (bf16[1,64000]{1,0:T(2,128)(2,1)S(1)}, bf16[1,64000]{1,0:T(2,128)(2,1)S(1)}, u32[]{:S(2)}, u32[]{:S(2)}) collective-permute-start(bf16[1,64000]{1,0:T(2,128)(2,1)S(1)} %copy-done.2), channel_id=1, source_target_pairs={{0,16},{16,32},{32,48},{48,64},{64,80},{80,96},{96,112},{112,128},... | collective-permute-start | bytes 384008 | tf_op jit(solution)/shard_map/ppermute | solution.py:342
  23.3 3.1 %collective-permute-start.1 = (bf16[1,64000]{1,0:T(2,128)(2,1)S(1)}, bf16[1,64000]{1,0:T(2,128)(2,1)S(1)}, u32[]{:S(2)}, u32[]{:S(2)}) collective-permute-start(bf16[1,64000]{1,0:T(2,128)(2,1)S(1)} %copy-done.2), channel_id=1, source_target_pairs={{0,32},{16,48},{32,64},{48,80},{64,96},{80,112},{96,128},{112,144}... | collective-permute-start | bytes 384008 | tf_op jit(solution)/shard_map/ppermute | solution.py:342
  26.4 0.6 reshape.38.o_ref
  27.0 2.6 %collective-permute-done = bf16[1,64000]{1,0:T(2,128)(2,1)S(1)} collective-permute-done((bf16[1,64000]{1,0:T(2,128)(2,1)S(1)}, bf16[1,64000]{1,0:T(2,128)(2,1)S(1)}, u32[]{:S(2)}, u32[]{:S(2)}) %collective-permute-start) | collective-permute-done | bytes 128032 | tf_op jit(solution)/shard_map/ppermute | solution.py:342
  29.6 0.7 reduce.1
  30.4 0.6 reshape.39.a_ref
  31.0 0.0 copy-start
  31.0 19.8 %collective-permute-done.1 = bf16[1,64000]{1,0:T(2,128)(2,1)S(1)} collective-permute-done((bf16[1,64000]{1,0:T(2,128)(2,1)S(1)}, bf16[1,64000]{1,0:T(2,128)(2,1)S(1)}, u32[]{:S(2)}, u32[]{:S(2)}) %collective-permute-start.1) | collective-permute-done | bytes 128032 | tf_op jit(solution)/shard_map/ppermute | solution.py:342
  50.8 0.8 reduce.2
  51.5 0.0 copy-start.1
  51.6 0.6 reshape.40.b_ref
  52.2 0.2 copy-done.1
  52.4 6.7 %exchange.1 = bf16[1600,40]{1,0:T(8,128)(2,1)S(1)} custom-call(bf16[1600,40]{1,0:T(8,128)(2,1)S(1)} %reshape.38.o_ref, bf16[1600,40]{1,0:T(8,128)(2,1)S(1)} %reshape.39.a_ref, bf16[1600,40]{1,0:T(8,128)(2,1)S(1)} %reshape.40.b_ref, bf16[2,128,128]{2,1,0:T(8,128)(2,1)S(1)} %copy-done.1, f32[21,40,128]{2,1,0:T(8,128)S(1)} %copy-done), custom_call_target="tpu_custom_call" | custom-call | flops 10000000 | bytes 4000000 | tf_op jit(solution)/shard_map/exchange/pallas_call | solution.py:172
  59.1 0.4 broadcast_in_dim.20
  59.5 0.1 broadcast_in_dim.21
  59.6 1.3 copy.19
  60.9 9.4 %all-to-all-start = ((bf16[128,2,1000]{2,1,0:T(2,128)(2,1)}), bf16[128,2,1000]{2,1,0:T(2,128)(2,1)S(1)}, u32[]{:S(2)}, u32[]{:S(2)}) async-start(bf16[128,2,1000]{2,1,0:T(2,128)(2,1)} %copy.19), calls=%async_computation | async-start | bytes 1048576 | tf_op jit(solution)/shard_map/all_to_all | solution.py:346
  70.3 0.4 copy.20
  70.7 0.6 reshape.44
  71.3 18.4 %all-to-all-done = bf16[128,2,1000]{2,1,0:T(2,128)(2,1)S(1)} async-done(((bf16[128,2,1000]{2,1,0:T(2,128)(2,1)}), bf16[128,2,1000]{2,1,0:T(2,128)(2,1)S(1)}, u32[]{:S(2)}, u32[]{:S(2)}) %all-to-all-start) | async-done | bytes 512032 | tf_op jit(solution)/shard_map/all_to_all | solution.py:346
  89.7 0.6 dot_general.17
  90.3 0.3 fusion.2
  90.6 7.2 %all_to_all.30 = f32[4,32,128]{2,1,0:T(8,128)S(1)} all-to-all(f32[4,32,128]{2,1,0:T(8,128)S(1)} %fusion.2), channel_id=1, replica_groups=mesh['yh'=4,'x'=4,'c'=2,'yl'=2,'z'=8] {'c','yl'}, dimensions={0} | all-to-all | bytes 131072 | tf_op jit(solution)/shard_map/all_to_all | solution.py:346
  97.8 10.8 %all_to_all.31 = f32[8,32,128]{2,1,0:T(8,128)S(1)} all-to-all(f32[8,32,128]{2,1,0:T(8,128)S(1)} %broadcast_in_dim.24), channel_id=1, replica_groups=mesh['yh'=4,'x'=4,'c'=2,'yl'=2,'z'=8] {'z'}, dimensions={0} | all-to-all | bytes 262144 | tf_op jit(solution)/shard_map/all_to_all | solution.py:346
  108.6 0.1 broadcast_in_dim.25
  108.7 16.7 %all_to_all.32 = f32[32,32,128]{2,1,0:T(8,128)S(1)} all-to-all(f32[32,32,128]{2,1,0:T(8,128)S(1)} %broadcast_in_dim.25), channel_id=1, replica_groups=mesh['yh'=4,'x'=4,'c'=2,'yl'=2,'z'=8] {'yh','x','yl'}, dimensions={0} | all-to-all | bytes 1048576 | tf_op jit(solution)/shard_map/all_to_all | solution.py:346
  125.3 6.7 %collective-permute-start.2 = (f32[16,64,128]{2,1,0:T(8,128)S(1)}, f32[16,64,128]{2,1,0:T(8,128)S(1)}, u32[]{:S(2)}, u32[]{:S(2)}) collective-permute-start(f32[16,64,128]{2,1,0:T(8,128)S(1)} %bitcast.35), channel_id=1, source_target_pairs={{0,16},{16,0},{1,17},{17,1},{2,18},{18,2},{3,19},{19,3},{4,20},{20... | collective-permute-start | bytes 1572872 | tf_op jit(solution)/shard_map/ppermute | solution.py:342
  132.1 0.7 copy.22
  132.8 4.1 %collective-permute-start.5 = (bf16[128,2000]{0,1:T(8,128)(2,1)S(1)}, bf16[128,2000]{0,1:T(8,128)(2,1)S(1)}, u32[]{:S(2)}, u32[]{:S(2)}) collective-permute-start(bf16[128,2000]{0,1:T(8,128)(2,1)S(1)} %bitcast.37), channel_id=1, source_target_pairs={{0,96},{32,0},{64,32},{96,64},{1,97},{33,1},{65,33},{97,65},{2,98}... | collective-permute-start | bytes 1536008 | tf_op jit(solution)/shard_map/ppermute | solution.py:342
  136.9 0.1 pad_add_fusion.place_ref
  137.0 1.9 %collective-permute-start.3 = (bf16[128,2000]{0,1:T(8,128)(2,1)S(1)}, bf16[128,2000]{0,1:T(8,128)(2,1)S(1)}, u32[]{:S(2)}, u32[]{:S(2)}) collective-permute-start(bf16[128,2000]{0,1:T(8,128)(2,1)S(1)} %bitcast.38), channel_id=1, source_target_pairs={{0,32},{32,64},{64,96},{96,0},{1,33},{33,65},{65,97},{97,1},{2,34}... | collective-permute-start | bytes 1536008 | tf_op jit(solution)/shard_map/ppermute | solution.py:342
  138.9 3.6 %collective-permute-start.4 = (bf16[128,2000]{0,1:T(8,128)(2,1)S(1)}, bf16[128,2000]{0,1:T(8,128)(2,1)S(1)}, u32[]{:S(2)}, u32[]{:S(2)}) collective-permute-start(bf16[128,2000]{0,1:T(8,128)(2,1)S(1)} %bitcast.39), channel_id=1, source_target_pairs={{0,64},{32,96},{64,0},{96,32},{1,65},{33,97},{65,1},{97,33},{2,66}... | collective-permute-start | bytes 1536008 | tf_op jit(solution)/shard_map/ppermute | solution.py:342
  142.5 0.1 pad_maximum_fusion.parts_ref
  142.6 15.5 %factor.1 = bf16[4,32,128]{2,1,0:T(8,128)(2,1)S(1)} custom-call(s32[4]{0:T(128)S(1)} %pad_add_fusion.place_ref, f32[2,16,64,128]{3,2,1,0:T(8,128)S(1)} %pad_maximum_fusion.parts_ref), custom_call_target="tpu_custom_call" | custom-call | flops 400000000 | bytes 4000000 | tf_op jit(solution)/shard_map/factor/pallas_call | solution.py:321
  158.2 0.3 fusion.5
  158.4 0.2 collective-permute-done.5
  158.7 0.3 fusion.4
  159.0 5.0 %collective-permute-done.3 = bf16[128,2000]{0,1:T(8,128)(2,1)S(1)} collective-permute-done((bf16[128,2000]{0,1:T(8,128)(2,1)S(1)}, bf16[128,2000]{0,1:T(8,128)(2,1)S(1)}, u32[]{:S(2)}, u32[]{:S(2)}) %collective-permute-start.3) | collective-permute-done | bytes 512032 | tf_op jit(solution)/shard_map/ppermute | solution.py:342
  163.9 0.3 convolution_add_fusion.1
  164.2 0.0 collective-permute-done.4
  164.3 0.3 fusion.1
  164.6 0.2 reshape.47
  164.8 12.5 %all_to_all.33 = bf16[32,2,1000]{2,1,0:T(2,128)(2,1)S(1)} all-to-all(bf16[32,2,1000]{2,1,0:T(2,128)(2,1)S(1)} %reshape.47), channel_id=1, replica_groups=mesh['yh'=4,'x'=4,'c'=2,'yl'=2,'z'=8] {'c','yl','z'}, dimensions={0} | all-to-all | bytes 256000 | tf_op jit(solution)/shard_map/all_to_all | solution.py:346
  177.2 1.0 reshape.48
  (9 shorter events, 0.1 us)
Async XLA Ops:
  2.9 17.1 %copy-start.2 = (bf16[1,64000]{1,0:T(2,128)(2,1)S(1)}, bf16[1,64000]{1,0:T(2,128)(2,1)}, u32[]{:S(2)}) copy-start(bf16[1,64000]{1,0:T(2,128)(2,1)} %param.3) | copy-start | bytes 384004
  2.9 58.0 %all-to-all-start.1 = ((bf16[128,2,1000]{2,1,0:T(2,128)(2,1)}), bf16[128,2,1000]{2,1,0:T(2,128)(2,1)S(1)}, u32[]{:S(2)}, u32[]{:S(2)}) async-start(bf16[128,2,1000]{2,1,0:T(2,128)(2,1)} %bitcast.5), calls=%async_computation.1 | async-start | bytes 1048576 | tf_op jit(solution)/shard_map/all_to_all | solution.py:346
  20.0 9.6 %collective-permute-start = (bf16[1,64000]{1,0:T(2,128)(2,1)S(1)}, bf16[1,64000]{1,0:T(2,128)(2,1)S(1)}, u32[]{:S(2)}, u32[]{:S(2)}) collective-permute-start(bf16[1,64000]{1,0:T(2,128)(2,1)S(1)} %copy-done.2), channel_id=1, source_target_pairs={{0,16},{16,32},{32,48},{48,64},{64,80},{80,96},{96,112},{112,128},... | collective-permute-start | bytes 384008 | tf_op jit(solution)/shard_map/ppermute | solution.py:342
  23.3 27.5 %collective-permute-start.1 = (bf16[1,64000]{1,0:T(2,128)(2,1)S(1)}, bf16[1,64000]{1,0:T(2,128)(2,1)S(1)}, u32[]{:S(2)}, u32[]{:S(2)}) collective-permute-start(bf16[1,64000]{1,0:T(2,128)(2,1)S(1)} %copy-done.2), channel_id=1, source_target_pairs={{0,32},{16,48},{32,64},{48,80},{64,96},{80,112},{96,128},{112,144}... | collective-permute-start | bytes 384008 | tf_op jit(solution)/shard_map/ppermute | solution.py:342
  31.0 21.2 %copy-start = (f32[21,40,128]{2,1,0:T(8,128)S(1)}, f32[21,40,128]{2,1,0:T(8,128)}, u32[]{:S(2)}) copy-start(f32[21,40,128]{2,1,0:T(8,128)} %constant.25.clone.kernel_ref) | copy-start | bytes 1290244
  51.5 0.8 copy-start.1
  60.9 28.8 %all-to-all-start = ((bf16[128,2,1000]{2,1,0:T(2,128)(2,1)}), bf16[128,2,1000]{2,1,0:T(2,128)(2,1)S(1)}, u32[]{:S(2)}, u32[]{:S(2)}) async-start(bf16[128,2,1000]{2,1,0:T(2,128)(2,1)} %copy.19), calls=%async_computation | async-start | bytes 1048576 | tf_op jit(solution)/shard_map/all_to_all | solution.py:346
  125.3 17.2 %collective-permute-start.2 = (f32[16,64,128]{2,1,0:T(8,128)S(1)}, f32[16,64,128]{2,1,0:T(8,128)S(1)}, u32[]{:S(2)}, u32[]{:S(2)}) collective-permute-start(f32[16,64,128]{2,1,0:T(8,128)S(1)} %bitcast.35), channel_id=1, source_target_pairs={{0,16},{16,0},{1,17},{17,1},{2,18},{18,2},{3,19},{19,3},{4,20},{20... | collective-permute-start | bytes 1572872 | tf_op jit(solution)/shard_map/ppermute | solution.py:342
  132.8 25.9 %collective-permute-start.5 = (bf16[128,2000]{0,1:T(8,128)(2,1)S(1)}, bf16[128,2000]{0,1:T(8,128)(2,1)S(1)}, u32[]{:S(2)}, u32[]{:S(2)}) collective-permute-start(bf16[128,2000]{0,1:T(8,128)(2,1)S(1)} %bitcast.37), channel_id=1, source_target_pairs={{0,96},{32,0},{64,32},{96,64},{1,97},{33,1},{65,33},{97,65},{2,98}... | collective-permute-start | bytes 1536008 | tf_op jit(solution)/shard_map/ppermute | solution.py:342
  137.0 27.0 %collective-permute-start.3 = (bf16[128,2000]{0,1:T(8,128)(2,1)S(1)}, bf16[128,2000]{0,1:T(8,128)(2,1)S(1)}, u32[]{:S(2)}, u32[]{:S(2)}) collective-permute-start(bf16[128,2000]{0,1:T(8,128)(2,1)S(1)} %bitcast.38), channel_id=1, source_target_pairs={{0,32},{32,64},{64,96},{96,0},{1,33},{33,65},{65,97},{97,1},{2,34}... | collective-permute-start | bytes 1536008 | tf_op jit(solution)/shard_map/ppermute | solution.py:342
  138.9 25.4 %collective-permute-start.4 = (bf16[128,2000]{0,1:T(8,128)(2,1)S(1)}, bf16[128,2000]{0,1:T(8,128)(2,1)S(1)}, u32[]{:S(2)}, u32[]{:S(2)}) collective-permute-start(bf16[128,2000]{0,1:T(8,128)(2,1)S(1)} %bitcast.39), channel_id=1, source_target_pairs={{0,64},{32,96},{64,0},{96,32},{1,65},{33,97},{65,1},{97,33},{2,66}... | collective-permute-start | bytes 1536008 | tf_op jit(solution)/shard_map/ppermute | solution.py:342
